TPU v7x, 32 devices: a whole 2x2x4 slice. The times are simulated.
32 devices in a mesh: row: 8 (over y, x, core), col: 4 (over z).
Axes of the slice: x: 2, y: 2, z: 4, core: 2. Of those that a mesh axis runs over, the one named last changes fastest.
Arguments:
- tiles: bfloat16 [128, 64, 128, 128], P('row', 'col'), may hold values from -0.09375 to 0.09375
- col_index: int32 [128, 64], P('row', 'col'), may hold values from 0 to 15
- counts: int32 [128, 4], P('row', 'col'), may hold values from 1 to 16, as said below
- sketch: bfloat16 [8192, 512], P('col'), may hold values from -6 to 6
Outputs:
- basis: float32 [16384, 512], P(('row', 'col'))
- factor: float32 [512, 512], replicated
Inputs may be any that keep to these rules, and one draw needn't show every extreme that they name: Slots at or beyond counts hold values that are ignored. Some tile row fills all 16 slots of some ignition block.
All inputs are finite; a program needn't handle non-finite values.
Results may differ from a plain program's by a relative error of at most 0.003.
Values may be sent and summed in bfloat16 or wider, within the bound.
No kernel may reach another device: no remote copies, remote signals or barrier semaphores. Data moves between devices by JAX's collectives and lax.ppermute only.
A program may use at most 128 MiB of HBM per device.

v0:
```python
import jax
import jax.numpy as jnp
from jax import lax
from jax.sharding import PartitionSpec as P


def swapped(value, axis, distance):
    mask = 2**distance
    pairs = [(source, source ^ mask) for source in range(lax.axis_size(axis))]
    return lax.ppermute(value, axis, pairs)


def local(tiles, col_index, counts, sketch):
    tile_rows, slots, tile = (tiles.shape[0], tiles.shape[1], tiles.shape[2])
    width = sketch.shape[1]
    col_tiles = sketch.shape[0] // tile
    total_rows = tile_rows * tile * lax.axis_size("row")
    live = (jnp.arange(slots)[None, :] < counts).astype(jnp.bfloat16)
    live_float = live.astype(jnp.float32)
    share_rows = tile_rows * tile // lax.axis_size("col")

    def project_rows(x_tiles):
        many = share_rows * lax.axis_size("col") // tile
        picked = jnp.take(x_tiles, col_index, axis=0) * live[:, :, None, None]
        matrix_product = jnp.einsum(
            "rsab,rsbk->rak", tiles, picked, preferred_element_type=jnp.float32
        )
        return lax.psum_scatter(
            matrix_product.reshape(many * tile, width), "col", scatter_dimension=0, tiled=True
        )

    def orthonormal(panel):
        gram = jnp.dot(
            panel.T, panel, precision=lax.Precision.HIGHEST, preferred_element_type=jnp.float32
        )
        for level in range(lax.axis_size(("row", "col")).bit_length() - 1):
            gram = gram + swapped(gram, ("row", "col"), level)
        lower = jnp.linalg.cholesky(gram / total_rows)
        basis = lax.linalg.triangular_solve(
            lower, panel, left_side=False, lower=True, transpose_a=True
        )
        return (basis, lower.T)

    first = project_rows(sketch.reshape(col_tiles, tile, width))
    first_q, unused = orthonormal(first)
    q_local = lax.all_gather(first_q.astype(jnp.bfloat16), "col", axis=0, tiled=True).reshape(
        tile_rows, tile, width
    )

    def accumulate(index, total):
        matrix_product = jnp.einsum(
            "sab,ak->sbk", tiles[index], q_local[index], preferred_element_type=jnp.float32
        )
        matrix_product = matrix_product * live_float[index][:, None, None]
        return total.at[col_index[index]].add(matrix_product)

    back_part = lax.fori_loop(
        0, tile_rows, accumulate, jnp.zeros((col_tiles, tile, width), jnp.float32)
    )
    back = lax.psum(back_part, "row").astype(jnp.bfloat16)
    second = project_rows(back)
    basis, factor = orthonormal(second)
    return (basis, factor)


def solution(mesh):
    return jax.shard_map(
        local,
        mesh=mesh,
        in_specs=(P("row", "col", None, None), P("row", "col"), P("row", "col"), P("col", None)),
        out_specs=(P(("row", "col"), None), P()),
        check_vma=False,
    )
```

profile of v0, /device:TPU:0, one launch (start us, length us, event | category | flops | bytes accessed | tf_op | source)
XLA Modules:
  0.0 1161.6 jit_solution(8305503465037512460)
XLA Ops:
  8.9 13.8 %gather_fusion = bf16[256,128,512]{2,1,0:T(8,128)(2,1)} fusion(bf16[16,128,512]{2,1,0:T(8,128)(2,1)S(1)} %bitcast.151, s32[1024]{0:T(1024)S(1)} %pad_clamp_fusion), kind=kCustom, calls=%fused_computation.clone | custom fusion | bytes 67109888 | tf_op jit(solution)/shard_map/jit(_take)/gather | solution.py:24
  22.7 19.1 %fusion.9 = f32[16,512,128,1]{1,2,3,0:T(8,128)} fusion(bf16[16,16,128,128]{3,2,1,0:T(8,128)(2,1)} %param.11, bf16[16,16,128,512]{3,2,1,0:T(8,128)(2,1)} %bitcast.153, pred[16,16]{1,0:T(8,128)(4,1)S(1)} %get-tuple-element.199, bf16[16,16]{1,0:T(8,128)(2,1)S(1)} %get-tuple-element.194), kind=kOutput, calls=%fused_computation.22 | convolution fusion | flops 4378853376 | bytes 46138112 | tf_op jit(solution)/shard_map/rsab,rsbk->rak/dot_general | solution.py:25
  42.0 79.5 %reduce-scatter.3.cloned.1.call-done = f32[512,512]{1,0:T(8,128)} async-done(((f32[2048,512]{1,0:T(8,128)}), f32[512,512]{1,0:T(8,128)}) %reduce-scatter.3.cloned.1.call-update) | async-done | bytes 1048592 | tf_op jit(solution)/shard_map/reduce_scatter | solution.py:28
  126.5 23.1 %collective-permute-done = f32[512,512]{0,1:T(8,128)S(1)} collective-permute-done((f32[512,512]{0,1:T(8,128)S(1)}, f32[512,512]{0,1:T(8,128)S(1)}, u32[]{:S(2)}, u32[]{:S(2)}) %collective-permute-start) | collective-permute-done | bytes 1048608 | tf_op jit(solution)/shard_map/ppermute | solution.py:10
  153.1 44.7 %collective-permute-done.1 = f32[512,512]{0,1:T(8,128)S(1)} collective-permute-done((f32[512,512]{0,1:T(8,128)S(1)}, f32[512,512]{0,1:T(8,128)S(1)}, u32[]{:S(2)}, u32[]{:S(2)}) %collective-permute-start.1) | collective-permute-done | bytes 1048608 | tf_op jit(solution)/shard_map/ppermute | solution.py:10
  202.5 23.7 %collective-permute-done.3 = f32[512,512]{0,1:T(8,128)S(1)} collective-permute-done((f32[512,512]{0,1:T(8,128)S(1)}, f32[512,512]{0,1:T(8,128)S(1)}, u32[]{:S(2)}, u32[]{:S(2)}) %collective-permute-start.3) | collective-permute-done | bytes 1048608 | tf_op jit(solution)/shard_map/ppermute | solution.py:10
  227.9 23.0 %collective-permute-done.4 = f32[512,512]{0,1:T(8,128)} collective-permute-done((f32[512,512]{0,1:T(8,128)S(1)}, f32[512,512]{0,1:T(8,128)}, u32[]{:S(2)}, u32[]{:S(2)}) %collective-permute-start.4) | collective-permute-done | bytes 1048608 | tf_op jit(solution)/shard_map/ppermute | solution.py:10
  254.0 11.7 %cholesky.286 = f32[128,128]{1,0:T(8,128)S(1)} custom-call(f32[128,128]{1,0:T(8,128)S(1)} %cholesky.426), custom_call_target="Cholesky" | custom-call | tf_op jit(solution)/shard_map/jit(cholesky)/cholesky | solution.py:38
  265.8 9.8 custom-call.27
  278.2 12.1 %cholesky.305 = f32[128,128]{1,0:T(8,128)S(1)} custom-call(f32[128,128]{1,0:T(8,128)S(1)} %cholesky.430), custom_call_target="Cholesky" | custom-call | tf_op jit(solution)/shard_map/jit(cholesky)/cholesky | solution.py:38
  291.7 9.8 custom-call.28
  303.1 11.7 %cholesky.326 = f32[128,128]{1,0:T(8,128)S(1)} custom-call(f32[128,128]{1,0:T(8,128)S(1)} %cholesky.435), custom_call_target="Cholesky" | custom-call | tf_op jit(solution)/shard_map/jit(cholesky)/cholesky | solution.py:38
  315.5 9.8 custom-call.29
  326.7 11.9 %cholesky.343 = f32[128,128]{1,0:T(8,128)S(1)} custom-call(f32[128,128]{1,0:T(8,128)S(1)} %convolution_subtract_fusion.11), custom_call_target="Cholesky" | custom-call | tf_op jit(solution)/shard_map/jit(cholesky)/cholesky | solution.py:38
  342.0 8.5 while.18
  350.5 39.3 %custom-call.30 = f32[4,128,128]{1,2,0:T(8,128)S(1)} custom-call(f32[4,128,128]{2,1,0:T(8,128)S(1)} %get-tuple-element.129), custom_call_target="InvertDiagBlocksLowerTriangular" | custom-call | tf_op jit(solution)/shard_map/triangular_solve/custom-call.3 | solution.py:39
  395.5 45.8 %all-gather.2.cloned.1.call-done = bf16[2048,512]{0,1:T(8,128)(2,1)} async-done(((bf16[512,512]{0,1:T(8,128)(2,1)}), bf16[2048,512]{0,1:T(8,128)(2,1)}) %all-gather.2.cloned.1.call-update) | async-done | bytes 2097168 | tf_op jit(solution)/shard_map/all_gather | solution.py:46
  446.7 221.1 %while.17 = (s32[]{:T(128)}, f32[16,128,512]{2,1,0:T(8,128)}, s32[16,16]{1,0:T(8,128)}, bf16[16,16,128,128]{3,2,1,0:T(8,128)(2,1)}, bf16[16,128,512]{2,1,0:T(8,128)(2,1)S(1)}, /*index=5*/f32[16,16]{1,0:T(8,128)S(1)}, s32[]{:T(128)}) while((s32[]{:T(128)}, f32[16,128,512]{2,1,0:T(8,128)}, s32[16,16]{1,0:T(8,128)}, ...), condition=%wide.region_11.15_spmd, body=%wide.region_9.14_spmd.sunk | while | flops 270532672 | bytes 17434516 | solution.py:57
  446.7 3.7 convolution_multiply_fusion.2
  451.1 9.4 scatter_fusion
  460.5 3.7 convolution_multiply_fusion.2
  464.9 9.5 scatter_fusion
  474.4 3.7 convolution_multiply_fusion.2
  478.8 9.3 scatter_fusion
  488.1 3.7 convolution_multiply_fusion.2
  492.5 9.3 scatter_fusion
  501.8 3.7 convolution_multiply_fusion.2
  506.2 9.5 scatter_fusion
  515.7 3.7 convolution_multiply_fusion.2
  520.1 9.7 scatter_fusion
  529.8 3.7 convolution_multiply_fusion.2
  534.2 9.4 scatter_fusion
  548.0 9.4 scatter_fusion
  557.4 3.7 convolution_multiply_fusion.2
  561.8 9.2 scatter_fusion
  571.0 3.7 convolution_multiply_fusion.2
  575.4 9.4 scatter_fusion
  584.8 3.7 convolution_multiply_fusion.2
  589.2 9.4 scatter_fusion
  598.6 3.7 convolution_multiply_fusion.2
  603.0 9.4 scatter_fusion
  616.8 9.4 scatter_fusion
  630.5 9.5 scatter_fusion
  640.0 3.7 convolution_multiply_fusion.2
  644.4 9.4 scatter_fusion
  653.8 3.7 convolution_multiply_fusion.2
  658.3 9.6 scatter_fusion
  667.8 88.4 %all-reduce.2 = bf16[16,128,512]{2,1,0:T(8,128)(2,1)S(1)} all-reduce(f32[16,128,512]{2,1,0:T(8,128)} %get-tuple-element.114), channel_id=1, replica_groups=mesh['row'=8,'col'=4] {'row'}, use_global_device_ids=true, to_apply=%region_12.16 | all-reduce | flops 1048576 | bytes 6291456 | tf_op jit(solution)/shard_map/psum | solution.py:60
  756.2 13.8 %gather_fusion.1 = bf16[256,128,512]{2,1,0:T(8,128)(2,1)} fusion(bf16[16,128,512]{2,1,0:T(8,128)(2,1)S(1)} %all-reduce.2, s32[1024]{0:T(1024)S(1)} %pad_clamp_fusion), kind=kCustom, calls=%fused_computation.1.clone | custom fusion | bytes 67109888 | tf_op jit(solution)/shard_map/jit(_take)/gather | solution.py:24
  770.0 19.4 %fusion.8 = f32[16,512,128,1]{1,2,3,0:T(8,128)} fusion(bf16[16,16,128,128]{3,2,1,0:T(8,128)(2,1)} %get-tuple-element.379, bf16[16,16,128,512]{3,2,1,0:T(8,128)(2,1)} %bitcast.152, pred[16,16]{1,0:T(8,128)(4,1)S(1)} %get-tuple-element.199, bf16[16,16]{1,0:T(8,128)(2,1)S(1)} %get-tuple-element.194), kind=kOutput, calls=%fused_computation.20 | convolution fusion | flops 4378853376 | bytes 46138112 | tf_op jit(solution)/shard_map/rsab,rsbk->rak/dot_general | solution.py:25
  789.5 75.0 %reduce-scatter.5.cloned.1.call-done = f32[512,512]{1,0:T(8,128)} async-done(((f32[2048,512]{1,0:T(8,128)}), f32[512,512]{1,0:T(8,128)}) %reduce-scatter.5.cloned.1.call-update) | async-done | bytes 1048592 | tf_op jit(solution)/shard_map/reduce_scatter | solution.py:28
  869.5 23.1 %collective-permute-done.5 = f32[512,512]{0,1:T(8,128)S(1)} collective-permute-done((f32[512,512]{0,1:T(8,128)S(1)}, f32[512,512]{0,1:T(8,128)S(1)}, u32[]{:S(2)}, u32[]{:S(2)}) %collective-permute-start.5) | collective-permute-done | bytes 1048608 | tf_op jit(solution)/shard_map/ppermute | solution.py:10
  896.1 44.7 %collective-permute-done.6 = f32[512,512]{0,1:T(8,128)S(1)} collective-permute-done((f32[512,512]{0,1:T(8,128)S(1)}, f32[512,512]{0,1:T(8,128)S(1)}, u32[]{:S(2)}, u32[]{:S(2)}) %collective-permute-start.6) | collective-permute-done | bytes 1048608 | tf_op jit(solution)/shard_map/ppermute | solution.py:10
  945.5 23.7 %collective-permute-done.8 = f32[512,512]{0,1:T(8,128)S(1)} collective-permute-done((f32[512,512]{0,1:T(8,128)S(1)}, f32[512,512]{0,1:T(8,128)S(1)}, u32[]{:S(2)}, u32[]{:S(2)}) %collective-permute-start.8) | collective-permute-done | bytes 1048608 | tf_op jit(solution)/shard_map/ppermute | solution.py:10
  971.0 22.9 %collective-permute-done.9 = f32[512,512]{0,1:T(8,128)S(1)} collective-permute-done((f32[512,512]{0,1:T(8,128)S(1)}, f32[512,512]{0,1:T(8,128)S(1)}, u32[]{:S(2)}, u32[]{:S(2)}) %collective-permute-start.9) | collective-permute-done | bytes 1048608 | tf_op jit(solution)/shard_map/ppermute | solution.py:10
  995.6 11.7 %cholesky.358 = f32[128,128]{1,0:T(8,128)S(1)} custom-call(f32[128,128]{1,0:T(8,128)S(1)} %cholesky.439), custom_call_target="Cholesky" | custom-call | tf_op jit(solution)/shard_map/jit(cholesky)/cholesky | solution.py:38
  1008.4 9.8 custom-call.31
  1021.4 11.9 %cholesky.377 = f32[128,128]{1,0:T(8,128)S(1)} custom-call(f32[128,128]{1,0:T(8,128)S(1)} %cholesky.443), custom_call_target="Cholesky" | custom-call | tf_op jit(solution)/shard_map/jit(cholesky)/cholesky | solution.py:38
  1035.3 9.8 custom-call.32
  1047.5 11.7 %cholesky.398 = f32[128,128]{1,0:T(8,128)S(1)} custom-call(f32[128,128]{1,0:T(8,128)S(1)} %cholesky.448), custom_call_target="Cholesky" | custom-call | tf_op jit(solution)/shard_map/jit(cholesky)/cholesky | solution.py:38
  1060.5 9.8 custom-call.33
  1072.6 11.9 %cholesky.415 = f32[128,128]{1,0:T(8,128)S(1)} custom-call(f32[128,128]{1,0:T(8,128)S(1)} %convolution_subtract_fusion.10), custom_call_target="Cholesky" | custom-call | tf_op jit(solution)/shard_map/jit(cholesky)/cholesky | solution.py:38
  1091.1 11.5 while.19
  1103.3 40.1 %custom-call.34 = f32[4,128,128]{1,2,0:T(8,128)S(1)} custom-call(f32[4,128,128]{2,1,0:T(8,128)} %copy-done.6), custom_call_target="InvertDiagBlocksLowerTriangular" | custom-call | tf_op jit(solution)/shard_map/triangular_solve/custom-call.3 | solution.py:39
  (173 shorter events, 126.4 us)
Async XLA Ops:
  7.2 1.8 copy-start
  7.2 114.3 %reduce-scatter.3.cloned.1.call-start = ((), (), s32[]{:S(2)}) async-start(), calls=%async_computation.2 | async-start | bytes 5242880 | tf_op jit(solution)/shard_map/reduce_scatter | solution.py:28
  41.8 399.5 %all-gather.2.cloned.1.call-start = ((), (), s32[]{:S(2)}) async-start(), calls=%async_computation.3 | async-start | bytes 2621440 | tf_op jit(solution)/shard_map/all_gather | solution.py:46
  124.9 24.7 %collective-permute-start = (f32[512,512]{0,1:T(8,128)S(1)}, f32[512,512]{0,1:T(8,128)S(1)}, u32[]{:S(2)}, u32[]{:S(2)}) collective-permute-start(f32[512,512]{0,1:T(8,128)S(1)} %fusion.93), channel_id=1, source_target_pairs={{0,1},{1,0},{2,3},{3,2},{4,5},{5,4},{6,7},{7,6},{8,9},{9,8},{10,11... | collective-permute-start | bytes 3145736 | tf_op jit(solution)/shard_map/ppermute | solution.py:10
  149.8 48.0 %collective-permute-start.1 = (f32[512,512]{0,1:T(8,128)S(1)}, f32[512,512]{0,1:T(8,128)S(1)}, u32[]{:S(2)}, u32[]{:S(2)}) collective-permute-start(f32[512,512]{0,1:T(8,128)S(1)} %add.113), channel_id=1, source_target_pairs={{0,2},{1,3},{2,0},{3,1},{4,6},{5,7},{6,4},{7,5},{8,10},{9,11},{10,... | collective-permute-start | bytes 3145736 | tf_op jit(solution)/shard_map/ppermute | solution.py:10
  198.0 2.7 collective-permute-start.2
  200.9 25.3 %collective-permute-start.3 = (f32[512,512]{0,1:T(8,128)S(1)}, f32[512,512]{0,1:T(8,128)S(1)}, u32[]{:S(2)}, u32[]{:S(2)}) collective-permute-start(f32[512,512]{0,1:T(8,128)S(1)} %add.115), channel_id=1, source_target_pairs={{0,8},{1,9},{2,10},{3,11},{4,12},{5,13},{6,14},{7,15},{8,0},{9,1},... | collective-permute-start | bytes 3145736 | tf_op jit(solution)/shard_map/ppermute | solution.py:10
  226.4 163.4 %copy-start.2 = (f32[512,512]{1,0:T(8,128)S(1)}, f32[512,512]{1,0:T(8,128)}, u32[]{:S(2)}) copy-start(f32[512,512]{1,0:T(8,128)} %reduce-scatter.3.cloned.1.call-done) | copy-start | bytes 3145732
  226.4 24.5 %collective-permute-start.4 = (f32[512,512]{0,1:T(8,128)S(1)}, f32[512,512]{0,1:T(8,128)}, u32[]{:S(2)}, u32[]{:S(2)}) collective-permute-start(f32[512,512]{0,1:T(8,128)S(1)} %add.116), channel_id=1, source_target_pairs={{0,16},{1,17},{2,18},{3,19},{4,20},{5,21},{6,22},{7,23},{8,24},{9,... | collective-permute-start | bytes 3145736 | tf_op jit(solution)/shard_map/ppermute | solution.py:10
  253.0 1.0 copy-start.4
  395.5 469.1 %reduce-scatter.5.cloned.1.call-start = ((), (), s32[]{:S(2)}) async-start(), calls=%async_computation.4 | async-start | bytes 5242880 | tf_op jit(solution)/shard_map/reduce_scatter | solution.py:28
  868.0 24.7 %collective-permute-start.5 = (f32[512,512]{0,1:T(8,128)S(1)}, f32[512,512]{0,1:T(8,128)S(1)}, u32[]{:S(2)}, u32[]{:S(2)}) collective-permute-start(f32[512,512]{0,1:T(8,128)S(1)} %fusion.94), channel_id=1, source_target_pairs={{0,1},{1,0},{2,3},{3,2},{4,5},{5,4},{6,7},{7,6},{8,9},{9,8},{10,11... | collective-permute-start | bytes 3145736 | tf_op jit(solution)/shard_map/ppermute | solution.py:10
  892.8 47.9 %collective-permute-start.6 = (f32[512,512]{0,1:T(8,128)S(1)}, f32[512,512]{0,1:T(8,128)S(1)}, u32[]{:S(2)}, u32[]{:S(2)}) collective-permute-start(f32[512,512]{0,1:T(8,128)S(1)} %add.118), channel_id=1, source_target_pairs={{0,2},{1,3},{2,0},{3,1},{4,6},{5,7},{6,4},{7,5},{8,10},{9,11},{10,... | collective-permute-start | bytes 3145736 | tf_op jit(solution)/shard_map/ppermute | solution.py:10
  941.0 2.7 collective-permute-start.7
  943.9 25.3 %collective-permute-start.8 = (f32[512,512]{0,1:T(8,128)S(1)}, f32[512,512]{0,1:T(8,128)S(1)}, u32[]{:S(2)}, u32[]{:S(2)}) collective-permute-start(f32[512,512]{0,1:T(8,128)S(1)} %add.120), channel_id=1, source_target_pairs={{0,8},{1,9},{2,10},{3,11},{4,12},{5,13},{6,14},{7,15},{8,0},{9,1},... | collective-permute-start | bytes 3145736 | tf_op jit(solution)/shard_map/ppermute | solution.py:10
  969.4 174.0 %copy-start.3 = (f32[512,512]{1,0:T(8,128)S(1)}, f32[512,512]{1,0:T(8,128)}, u32[]{:S(2)}) copy-start(f32[512,512]{1,0:T(8,128)} %reduce-scatter.5.cloned.1.call-done) | copy-start | bytes 3145732
  969.4 24.4 %collective-permute-start.9 = (f32[512,512]{0,1:T(8,128)S(1)}, f32[512,512]{0,1:T(8,128)S(1)}, u32[]{:S(2)}, u32[]{:S(2)}) collective-permute-start(f32[512,512]{0,1:T(8,128)S(1)} %add.121), channel_id=1, source_target_pairs={{0,16},{1,17},{2,18},{3,19},{4,20},{5,21},{6,22},{7,23},{8,24},{9,... | collective-permute-start | bytes 3145736 | tf_op jit(solution)/shard_map/ppermute | solution.py:10
  994.6 1.0 copy-start.5
  1070.3 84.5 %copy-start.1 = (bf16[2048,512]{1,0:T(8,128)(2,1)S(1)}, bf16[2048,512]{1,0:T(8,128)(2,1)}, u32[]{:S(2)}) copy-start(bf16[2048,512]{1,0:T(8,128)(2,1)} %param.14) | copy-start | bytes 6291460
  1102.6 0.7 copy-start.6
Sparse Core Ops, SparseCore 0:
  41.9 79.5 reduce-scatter.2
  395.6 45.7 all-gather.1
  789.6 74.8 reduce-scatter.4
where the time goes:
time: 1170 us; the launch traced here: 1160 us
  waiting for transfers between devices  435 us (37%)
  other arithmetic  411 us (35%)
  matrix products  130 us (11%)
  blocking collectives  88.4 us (8%)
  local copies, waits for them, and re-layouts  61.3 us (5%)
  between operations  19.6 us (2%)
  starting transfers between devices  16.2 us (1%)
    ppermute x10, waiting for transfers between devices, swapped(): return lax.ppermute(value, axis, pairs)  234 us
    another operation x30, other arithmetic, orthonormal(): lower = jnp.linalg.cholesky(gram / total_rows)  161 us
    reduce_scatter x2, waiting for transfers between devices, project_rows(): lax.psum_scatter(matrix_product.reshape(many * tile, width), 'col', scatt...  155 us
    scatter-add x16, other arithmetic, accumulate(): return total.at[col_index[index]].add(matrix_product)  151 us
    psum x1, blocking collectives, local(): back = lax.psum(back_part, 'row').astype(jnp.bfloat16)  88.4 us
    another operation x5, other arithmetic, orthonormal(): lax.linalg.triangular_solve(lower, panel, left_side=False, lower=True, tr...  79.6 us
    dot_general x16, matrix products, accumulate(): jnp.einsum('sab,ak->sbk', tiles[index], q_local[index], preferred_element...  59.4 us
    all_gather x1, waiting for transfers between devices, local(): lax.all_gather(first_q.astype(jnp.bfloat16), 'col', axis=0, tiled=True)  45.8 us
  transfers between devices with their start and end apart: 13, of which 13 were waited for; matrix products, arithmetic and copies ran while one was open for 0% of the time, Pallas kernels for 0%

commit v1 on v0

--- a/solution.py
+++ b/solution.py
@@ -57,7 +57,7 @@
     back_part = lax.fori_loop(
         0, tile_rows, accumulate, jnp.zeros((col_tiles, tile, width), jnp.float32)
     )
-    back = lax.psum(back_part, "row").astype(jnp.bfloat16)
+    back = jnp.sum(lax.all_gather(back_part, "row"), axis=0).astype(jnp.bfloat16)
     second = project_rows(back)
     basis, factor = orthonormal(second)
     return (basis, factor)

time: 1170 us -> 1260 us (1.077)
  waiting for transfers between devices: 435 us -> 598 us
  blocking collectives: 88.4 us -> 0 us
  other arithmetic: 411 us -> 424 us
    all_gather x0 -> x1, waiting for transfers between devices: none -> 161 us  [local(): lax.all_gather(back_part, 'row')]
    psum x1 -> x0, blocking collectives: 88.4 us -> none  [local(): back = lax.psum(back_part, 'row').astype(jnp.bfloat16)]
    reduce_sum x0 -> x1, other arithmetic: none -> 13.3 us  [local(): jnp.sum(lax.all_gather(back_part, 'row'), axis=0).astype(jnp.bfloat16)]
  transfers between devices with their start and end apart: 13 -> 14, of which waited for: 13 -> 14; matrix products, arithmetic and copies ran while one was open for 0% -> 0% of each run, Pallas kernels for 0% -> 0%
where the time goes in v1:
time: 1260 us; the launch traced here: 1250 us
  waiting for transfers between devices  598 us (47%)
  other arithmetic  424 us (34%)
  matrix products  130 us (10%)
  local copies, waits for them, and re-layouts  61.5 us (5%)
  between operations  19.6 us (2%)
  starting transfers between devices  16.2 us (1%)
    ppermute x10, waiting for transfers between devices, swapped(): return lax.ppermute(value, axis, pairs)  234 us
    all_gather x1, waiting for transfers between devices, local(): lax.all_gather(back_part, 'row')  161 us
    another operation x30, other arithmetic, orthonormal(): lower = jnp.linalg.cholesky(gram / total_rows)  161 us
    reduce_scatter x2, waiting for transfers between devices, project_rows(): lax.psum_scatter(matrix_product.reshape(many * tile, width), 'col', scatt...  156 us
    scatter-add x16, other arithmetic, accumulate(): return total.at[col_index[index]].add(matrix_product)  150 us
    another operation x5, other arithmetic, orthonormal(): lax.linalg.triangular_solve(lower, panel, left_side=False, lower=True, tr...  79.6 us
    dot_general x16, matrix products, accumulate(): jnp.einsum('sab,ak->sbk', tiles[index], q_local[index], preferred_element...  59.4 us
    all_gather x1, waiting for transfers between devices, local(): lax.all_gather(first_q.astype(jnp.bfloat16), 'col', axis=0, tiled=True)  45.8 us
  transfers between devices with their start and end apart: 14, of which 14 were waited for; matrix products, arithmetic and copies ran while one was open for 0% of the time, Pallas kernels for 0%

profile of v1, /device:TPU:0, one launch (start us, length us, event | category | flops | bytes accessed | tf_op | source)
XLA Modules:
  0.0 1249.6 jit_solution(14433400481700179065)
XLA Ops:
  8.9 13.8 %gather_fusion = bf16[256,128,512]{2,1,0:T(8,128)(2,1)} fusion(bf16[16,128,512]{2,1,0:T(8,128)(2,1)S(1)} %bitcast.152, s32[1024]{0:T(1024)S(1)} %pad_clamp_fusion), kind=kCustom, calls=%fused_computation.clone | custom fusion | bytes 67109888 | tf_op jit(solution)/shard_map/jit(_take)/gather | solution.py:24
  22.8 19.1 %fusion.9 = f32[16,512,128,1]{1,2,3,0:T(8,128)} fusion(bf16[16,16,128,128]{3,2,1,0:T(8,128)(2,1)} %param.11, bf16[16,16,128,512]{3,2,1,0:T(8,128)(2,1)} %bitcast.155, pred[16,16]{1,0:T(8,128)(4,1)S(1)} %get-tuple-element.207, bf16[16,16]{1,0:T(8,128)(2,1)S(1)} %get-tuple-element.202), kind=kOutput, calls=%fused_computation.22 | convolution fusion | flops 4378853376 | bytes 46138112 | tf_op jit(solution)/shard_map/rsab,rsbk->rak/dot_general | solution.py:25
  42.1 79.5 %reduce-scatter.3.cloned.1.call-done = f32[512,512]{1,0:T(8,128)} async-done(((f32[2048,512]{1,0:T(8,128)}), f32[512,512]{1,0:T(8,128)}) %reduce-scatter.3.cloned.1.call-update) | async-done | bytes 1048592 | tf_op jit(solution)/shard_map/reduce_scatter | solution.py:28
  126.5 23.1 %collective-permute-done = f32[512,512]{0,1:T(8,128)S(1)} collective-permute-done((f32[512,512]{0,1:T(8,128)S(1)}, f32[512,512]{0,1:T(8,128)S(1)}, u32[]{:S(2)}, u32[]{:S(2)}) %collective-permute-start) | collective-permute-done | bytes 1048608 | tf_op jit(solution)/shard_map/ppermute | solution.py:10
  153.1 44.7 %collective-permute-done.1 = f32[512,512]{0,1:T(8,128)S(1)} collective-permute-done((f32[512,512]{0,1:T(8,128)S(1)}, f32[512,512]{0,1:T(8,128)S(1)}, u32[]{:S(2)}, u32[]{:S(2)}) %collective-permute-start.1) | collective-permute-done | bytes 1048608 | tf_op jit(solution)/shard_map/ppermute | solution.py:10
  202.5 23.7 %collective-permute-done.3 = f32[512,512]{0,1:T(8,128)S(1)} collective-permute-done((f32[512,512]{0,1:T(8,128)S(1)}, f32[512,512]{0,1:T(8,128)S(1)}, u32[]{:S(2)}, u32[]{:S(2)}) %collective-permute-start.3) | collective-permute-done | bytes 1048608 | tf_op jit(solution)/shard_map/ppermute | solution.py:10
  228.0 23.0 %collective-permute-done.4 = f32[512,512]{0,1:T(8,128)} collective-permute-done((f32[512,512]{0,1:T(8,128)S(1)}, f32[512,512]{0,1:T(8,128)}, u32[]{:S(2)}, u32[]{:S(2)}) %collective-permute-start.4) | collective-permute-done | bytes 1048608 | tf_op jit(solution)/shard_map/ppermute | solution.py:10
  254.0 11.7 cholesky.286
  265.9 9.8 custom-call.27
  278.2 12.1 cholesky.305
  291.7 9.8 custom-call.28
  303.1 11.7 cholesky.326
  315.5 9.8 custom-call.29
  326.8 11.9 cholesky.343
  342.0 8.5 while.18
  350.5 39.3 %custom-call.30 = f32[4,128,128]{1,2,0:T(8,128)S(1)} custom-call(f32[4,128,128]{2,1,0:T(8,128)S(1)} %get-tuple-element.129), custom_call_target="InvertDiagBlocksLowerTriangular" | custom-call | tf_op jit(solution)/shard_map/triangular_solve/custom-call.3 | solution.py:39
  395.5 45.8 %all-gather.4.cloned.1.call-done = bf16[2048,512]{0,1:T(8,128)(2,1)} async-done(((bf16[512,512]{0,1:T(8,128)(2,1)}), bf16[2048,512]{0,1:T(8,128)(2,1)}) %all-gather.4.cloned.1.call-update) | async-done | bytes 2097168 | tf_op jit(solution)/shard_map/all_gather | solution.py:46
  446.8 221.1 %while.17 = (s32[]{:T(128)}, f32[16,128,512]{2,1,0:T(8,128)}, s32[16,16]{1,0:T(8,128)}, bf16[16,16,128,128]{3,2,1,0:T(8,128)(2,1)}, bf16[16,128,512]{2,1,0:T(8,128)(2,1)S(1)}, /*index=5*/f32[16,16]{1,0:T(8,128)S(1)}, s32[]{:T(128)}) while((s32[]{:T(128)}, f32[16,128,512]{2,1,0:T(8,128)}, s32[16,16]{1,0:T(8,128)}, ...), condition=%wide.region_11.15_spmd, body=%wide.region_9.14_spmd.sunk | while | flops 270532672 | bytes 17434516 | solution.py:57
  446.8 3.7 convolution_multiply_fusion.2
  451.2 9.4 scatter_fusion
  460.7 3.7 convolution_multiply_fusion.2
  465.1 9.5 scatter_fusion
  474.6 3.7 convolution_multiply_fusion.2
  479.0 9.3 scatter_fusion
  488.2 3.7 convolution_multiply_fusion.2
  492.6 9.4 scatter_fusion
  506.4 9.5 scatter_fusion
  515.9 3.7 convolution_multiply_fusion.2
  520.3 9.6 scatter_fusion
  529.9 3.7 convolution_multiply_fusion.2
  534.3 9.3 scatter_fusion
  543.6 3.7 convolution_multiply_fusion.2
  548.1 9.4 scatter_fusion
  557.5 3.7 convolution_multiply_fusion.2
  561.9 9.1 scatter_fusion
  575.4 9.4 scatter_fusion
  584.8 3.7 convolution_multiply_fusion.2
  589.3 9.4 scatter_fusion
  598.6 3.7 convolution_multiply_fusion.2
  603.0 9.4 scatter_fusion
  612.5 3.7 convolution_multiply_fusion.2
  616.9 9.3 scatter_fusion
  626.2 3.7 convolution_multiply_fusion.2
  630.6 9.5 scatter_fusion
  644.5 9.4 scatter_fusion
  658.4 9.5 scatter_fusion
  668.0 161.0 %all-gather.6.cloned.1.call-done = f32[128,128,512]{2,1,0:T(8,128)} async-done(((f32[16,128,512]{2,1,0:T(8,128)}), f32[128,128,512]{2,1,0:T(8,128)}) %all-gather.6.cloned.1.call-update) | async-done | bytes 33554448 | tf_op jit(solution)/shard_map/all_gather | solution.py:60
  828.9 13.3 %reduce_sum.9 = bf16[16,128,512]{2,1,0:T(8,128)(2,1)S(1)} reduce(f32[8,16,128,512]{3,2,1,0:T(8,128)} %bitcast.153, f32[]{:T(128)} %constant.143.clone.1), dimensions={0}, to_apply=%region_12.16 | reduce | flops 7340032 | bytes 35651588 | tf_op jit(solution)/shard_map/reduce_sum | solution.py:60
  842.2 13.8 %gather_fusion.1 = bf16[256,128,512]{2,1,0:T(8,128)(2,1)} fusion(bf16[16,128,512]{2,1,0:T(8,128)(2,1)S(1)} %reduce_sum.9, s32[1024]{0:T(1024)S(1)} %pad_clamp_fusion), kind=kCustom, calls=%fused_computation.1.clone | custom fusion | bytes 67109888 | tf_op jit(solution)/shard_map/jit(_take)/gather | solution.py:24
  856.0 19.4 %fusion.8 = f32[16,512,128,1]{1,2,3,0:T(8,128)} fusion(bf16[16,16,128,128]{3,2,1,0:T(8,128)(2,1)} %get-tuple-element.391, bf16[16,16,128,512]{3,2,1,0:T(8,128)(2,1)} %bitcast.154, pred[16,16]{1,0:T(8,128)(4,1)S(1)} %get-tuple-element.207, bf16[16,16]{1,0:T(8,128)(2,1)S(1)} %get-tuple-element.202), kind=kOutput, calls=%fused_computation.20 | convolution fusion | flops 4378853376 | bytes 46138112 | tf_op jit(solution)/shard_map/rsab,rsbk->rak/dot_general | solution.py:25
  875.5 77.0 %reduce-scatter.5.cloned.1.call-done = f32[512,512]{1,0:T(8,128)} async-done(((f32[2048,512]{1,0:T(8,128)}), f32[512,512]{1,0:T(8,128)}) %reduce-scatter.5.cloned.1.call-update) | async-done | bytes 1048592 | tf_op jit(solution)/shard_map/reduce_scatter | solution.py:28
  957.5 23.1 %collective-permute-done.5 = f32[512,512]{0,1:T(8,128)S(1)} collective-permute-done((f32[512,512]{0,1:T(8,128)S(1)}, f32[512,512]{0,1:T(8,128)S(1)}, u32[]{:S(2)}, u32[]{:S(2)}) %collective-permute-start.5) | collective-permute-done | bytes 1048608 | tf_op jit(solution)/shard_map/ppermute | solution.py:10
  984.0 44.7 %collective-permute-done.6 = f32[512,512]{0,1:T(8,128)S(1)} collective-permute-done((f32[512,512]{0,1:T(8,128)S(1)}, f32[512,512]{0,1:T(8,128)S(1)}, u32[]{:S(2)}, u32[]{:S(2)}) %collective-permute-start.6) | collective-permute-done | bytes 1048608 | tf_op jit(solution)/shard_map/ppermute | solution.py:10
  1033.4 23.7 %collective-permute-done.8 = f32[512,512]{0,1:T(8,128)S(1)} collective-permute-done((f32[512,512]{0,1:T(8,128)S(1)}, f32[512,512]{0,1:T(8,128)S(1)}, u32[]{:S(2)}, u32[]{:S(2)}) %collective-permute-start.8) | collective-permute-done | bytes 1048608 | tf_op jit(solution)/shard_map/ppermute | solution.py:10
  1058.9 22.9 %collective-permute-done.9 = f32[512,512]{0,1:T(8,128)S(1)} collective-permute-done((f32[512,512]{0,1:T(8,128)S(1)}, f32[512,512]{0,1:T(8,128)S(1)}, u32[]{:S(2)}, u32[]{:S(2)}) %collective-permute-start.9) | collective-permute-done | bytes 1048608 | tf_op jit(solution)/shard_map/ppermute | solution.py:10
  1083.5 11.7 cholesky.358
  1096.4 9.8 custom-call.31
  1109.4 11.9 cholesky.377
  1123.3 9.8 custom-call.32
  1135.4 11.7 cholesky.398
  1148.5 9.8 custom-call.33
  1160.5 11.9 cholesky.415
  1179.1 11.5 while.19
  1191.3 40.1 %custom-call.34 = f32[4,128,128]{1,2,0:T(8,128)S(1)} custom-call(f32[4,128,128]{2,1,0:T(8,128)} %copy-done.6), custom_call_target="InvertDiagBlocksLowerTriangular" | custom-call | tf_op jit(solution)/shard_map/triangular_solve/custom-call.3 | solution.py:39
  (176 shorter events, 130.2 us)
Async XLA Ops:
  7.2 1.8 copy-start
  7.2 114.4 %reduce-scatter.3.cloned.1.call-start = ((), (), s32[]{:S(2)}) async-start(), calls=%async_computation.2 | async-start | bytes 5242880 | tf_op jit(solution)/shard_map/reduce_scatter | solution.py:28
  41.9 399.5 %all-gather.4.cloned.1.call-start = ((), (), s32[]{:S(2)}) async-start(), calls=%async_computation.3 | async-start | bytes 2621440 | tf_op jit(solution)/shard_map/all_gather | solution.py:46
  125.0 24.7 %collective-permute-start = (f32[512,512]{0,1:T(8,128)S(1)}, f32[512,512]{0,1:T(8,128)S(1)}, u32[]{:S(2)}, u32[]{:S(2)}) collective-permute-start(f32[512,512]{0,1:T(8,128)S(1)} %fusion.93), channel_id=1, source_target_pairs={{0,1},{1,0},{2,3},{3,2},{4,5},{5,4},{6,7},{7,6},{8,9},{9,8},{10,11... | collective-permute-start | bytes 3145736 | tf_op jit(solution)/shard_map/ppermute | solution.py:10
  149.9 48.0 %collective-permute-start.1 = (f32[512,512]{0,1:T(8,128)S(1)}, f32[512,512]{0,1:T(8,128)S(1)}, u32[]{:S(2)}, u32[]{:S(2)}) collective-permute-start(f32[512,512]{0,1:T(8,128)S(1)} %add.111), channel_id=1, source_target_pairs={{0,2},{1,3},{2,0},{3,1},{4,6},{5,7},{6,4},{7,5},{8,10},{9,11},{10,... | collective-permute-start | bytes 3145736 | tf_op jit(solution)/shard_map/ppermute | solution.py:10
  198.0 2.7 collective-permute-start.2
  201.0 25.3 %collective-permute-start.3 = (f32[512,512]{0,1:T(8,128)S(1)}, f32[512,512]{0,1:T(8,128)S(1)}, u32[]{:S(2)}, u32[]{:S(2)}) collective-permute-start(f32[512,512]{0,1:T(8,128)S(1)} %add.113), channel_id=1, source_target_pairs={{0,8},{1,9},{2,10},{3,11},{4,12},{5,13},{6,14},{7,15},{8,0},{9,1},... | collective-permute-start | bytes 3145736 | tf_op jit(solution)/shard_map/ppermute | solution.py:10
  226.5 163.4 %copy-start.2 = (f32[512,512]{1,0:T(8,128)S(1)}, f32[512,512]{1,0:T(8,128)}, u32[]{:S(2)}) copy-start(f32[512,512]{1,0:T(8,128)} %reduce-scatter.3.cloned.1.call-done) | copy-start | bytes 3145732
  226.5 24.5 %collective-permute-start.4 = (f32[512,512]{0,1:T(8,128)S(1)}, f32[512,512]{0,1:T(8,128)}, u32[]{:S(2)}, u32[]{:S(2)}) collective-permute-start(f32[512,512]{0,1:T(8,128)S(1)} %add.114), channel_id=1, source_target_pairs={{0,16},{1,17},{2,18},{3,19},{4,20},{5,21},{6,22},{7,23},{8,24},{9,... | collective-permute-start | bytes 3145736 | tf_op jit(solution)/shard_map/ppermute | solution.py:10
  253.0 1.0 copy-start.4
  395.5 433.4 %all-gather.6.cloned.1.call-start = ((), (), s32[]{:S(2)}) async-start(), calls=%async_computation.5 | async-start | bytes 37748736 | tf_op jit(solution)/shard_map/all_gather | solution.py:60
  667.9 284.6 %reduce-scatter.5.cloned.1.call-start = ((), (), s32[]{:S(2)}) async-start(), calls=%async_computation.4 | async-start | bytes 5242880 | tf_op jit(solution)/shard_map/reduce_scatter | solution.py:28
  955.9 24.7 %collective-permute-start.5 = (f32[512,512]{0,1:T(8,128)S(1)}, f32[512,512]{0,1:T(8,128)S(1)}, u32[]{:S(2)}, u32[]{:S(2)}) collective-permute-start(f32[512,512]{0,1:T(8,128)S(1)} %fusion.94), channel_id=1, source_target_pairs={{0,1},{1,0},{2,3},{3,2},{4,5},{5,4},{6,7},{7,6},{8,9},{9,8},{10,11... | collective-permute-start | bytes 3145736 | tf_op jit(solution)/shard_map/ppermute | solution.py:10
  980.8 47.9 %collective-permute-start.6 = (f32[512,512]{0,1:T(8,128)S(1)}, f32[512,512]{0,1:T(8,128)S(1)}, u32[]{:S(2)}, u32[]{:S(2)}) collective-permute-start(f32[512,512]{0,1:T(8,128)S(1)} %add.116), channel_id=1, source_target_pairs={{0,2},{1,3},{2,0},{3,1},{4,6},{5,7},{6,4},{7,5},{8,10},{9,11},{10,... | collective-permute-start | bytes 3145736 | tf_op jit(solution)/shard_map/ppermute | solution.py:10
  1028.9 2.7 collective-permute-start.7
  1031.9 25.3 %collective-permute-start.8 = (f32[512,512]{0,1:T(8,128)S(1)}, f32[512,512]{0,1:T(8,128)S(1)}, u32[]{:S(2)}, u32[]{:S(2)}) collective-permute-start(f32[512,512]{0,1:T(8,128)S(1)} %add.118), channel_id=1, source_target_pairs={{0,8},{1,9},{2,10},{3,11},{4,12},{5,13},{6,14},{7,15},{8,0},{9,1},... | collective-permute-start | bytes 3145736 | tf_op jit(solution)/shard_map/ppermute | solution.py:10
  1057.3 174.0 %copy-start.3 = (f32[512,512]{1,0:T(8,128)S(1)}, f32[512,512]{1,0:T(8,128)}, u32[]{:S(2)}) copy-start(f32[512,512]{1,0:T(8,128)} %reduce-scatter.5.cloned.1.call-done) | copy-start | bytes 3145732
  1057.4 24.4 %collective-permute-start.9 = (f32[512,512]{0,1:T(8,128)S(1)}, f32[512,512]{0,1:T(8,128)S(1)}, u32[]{:S(2)}, u32[]{:S(2)}) collective-permute-start(f32[512,512]{0,1:T(8,128)S(1)} %add.119), channel_id=1, source_target_pairs={{0,16},{1,17},{2,18},{3,19},{4,20},{5,21},{6,22},{7,23},{8,24},{9,... | collective-permute-start | bytes 3145736 | tf_op jit(solution)/shard_map/ppermute | solution.py:10
  1082.6 1.0 copy-start.5
  1158.3 84.5 %copy-start.1 = (bf16[2048,512]{1,0:T(8,128)(2,1)S(1)}, bf16[2048,512]{1,0:T(8,128)(2,1)}, u32[]{:S(2)}) copy-start(bf16[2048,512]{1,0:T(8,128)(2,1)} %param.14) | copy-start | bytes 6291460
  1190.6 0.7 copy-start.6
Sparse Core Ops, SparseCore 0:
  42.0 79.5 reduce-scatter.2
  395.6 45.7 all-gather.3
  668.1 160.8 all-gather.5
  875.6 76.8 reduce-scatter.4
